TPU v7x, 32 devices: a whole 2x2x4 slice. The times are simulated.
32 devices in a mesh: groups: 2 (over x), dp: 16 (over z, y, core).
Axes of the slice: x: 2, y: 2, z: 4, core: 2. Of those that a mesh axis runs over, the one named last changes fastest.
Arguments:
- clips: bfloat16 [128, 4, 49, 1024], P(('groups', 'dp')), parts along dimension 0, may hold values from -6 to 6
- sign_seeds: int32 [128], P(('groups', 'dp')), parts along dimension 0, may hold values from 0 to 999999
- time_weight: bfloat16 [3, 1024, 1024], replicated, may hold values from -0.109375 to 0.109375
- proj_weight: bfloat16 [1024, 512], replicated, may hold values from -0.1875 to 0.1875
- captions: bfloat16 [640, 512], P(('groups', 'dp')), parts along dimension 0, may hold values from -6 to 6
- caption_rows: int32 [128, 5], P(('groups', 'dp')), parts along dimension 0, may hold values from 0 to 319, as said below
Outputs:
- new_delta: bfloat16 [128, 4, 49, 1024], P(('groups', 'dp')), parts along dimension 0
- clip_loss: float32 [128], P(('groups', 'dp')), parts along dimension 0
There are 2 independent parts, one for each index of `groups`. A program takes and returns all parts, laid end to end along the dimension named above; an argument that names none is the same for every part. Nothing has to cross between parts.
Inputs may be any that keep to these rules, and one draw needn't show every extreme that they name: `caption_rows`: the captions of the clips of one dp device are the 20 caption rows of that device; every caption row belongs to exactly one clip.
All inputs are finite; a program needn't handle non-finite values.
Results may differ from a plain program's by a relative error of at most 0.008.
Values may be sent and summed in bfloat16 or wider, within the bound.
No kernel may reach another device: no remote copies, remote signals or barrier semaphores. Data moves between devices by JAX's collectives and lax.ppermute only.
A program may use at most 64 MiB of HBM per device.

v0:
```python
import jax
import jax.numpy as jnp
from jax import lax
from jax.sharding import PartitionSpec as P

INV_TEMP = 1.0 / 0.07


def sign_field(seeds, frames, pix, chans):
    first = lax.broadcasted_iota(jnp.int32, (frames, pix, chans), 0)
    second = lax.broadcasted_iota(jnp.int32, (frames, pix, chans), 1)
    third = lax.broadcasted_iota(jnp.int32, (frames, pix, chans), 2)
    position = (first * pix + second) * chans + third
    mixed = seeds[:, None, None, None] * jnp.int32(-1640531535) + position[None] * jnp.int32(
        374761393
    )
    mixed = mixed ^ mixed >> 13
    mixed = mixed * jnp.int32(668265263)
    mixed = mixed ^ mixed >> 16
    chosen = mixed >> 7 & 1
    return 0.1 * (2 * chosen - 1).astype(jnp.float32)


def temporal(inputs, time_weight):
    frames = inputs.shape[1]
    chans = inputs.shape[3]
    padded = jnp.pad(inputs, ((0, 0), (1, 1), (0, 0), (0, 0)))
    result = jnp.zeros(inputs.shape, jnp.float32)
    for k in range(3):
        window = padded[:, k : k + frames].reshape(-1, chans)
        result = result + jnp.dot(
            window, time_weight[k], preferred_element_type=jnp.float32
        ).reshape(inputs.shape)
    return result


def temporal_back(grad_pre, time_weight):
    frames = grad_pre.shape[1]
    chans = grad_pre.shape[3]
    padded = jnp.pad(grad_pre, ((0, 0), (1, 1), (0, 0), (0, 0)))
    result = jnp.zeros(grad_pre.shape, jnp.float32)
    for k in range(3):
        window = padded[:, 2 - k : 2 - k + frames].reshape(-1, chans)
        result = result + jnp.dot(
            window, time_weight[k].T, preferred_element_type=jnp.float32
        ).reshape(grad_pre.shape)
    return result


def gelu_tanh(value):
    return jax.nn.gelu(value, approximate=True)


def shards(clips, sign_seeds, time_weight, proj_weight, captions, caption_rows):
    clip_dev, frames, pix, chans = clips.shape
    caps_dev = captions.shape[0]
    delta0 = sign_field(sign_seeds, frames, pix, chans)
    inputs = (clips.astype(jnp.float32) + delta0).astype(jnp.bfloat16)
    pre = temporal(inputs, time_weight)
    active, act_back = jax.vjp(gelu_tanh, pre)
    pooled = jnp.mean(active, axis=(1, 2)).astype(jnp.bfloat16)
    video = jnp.dot(pooled, proj_weight, preferred_element_type=jnp.float32)
    vnorm = jnp.sqrt(jnp.sum(video * video, axis=1, keepdims=True) + 1e-06)
    vunit = video / vnorm
    video_hat = vunit.astype(jnp.bfloat16)
    cap32 = captions.astype(jnp.float32)
    caption_hat = (cap32 / jnp.sqrt(jnp.sum(cap32 * cap32, axis=1, keepdims=True) + 1e-06)).astype(
        jnp.bfloat16
    )
    local_rows = caption_rows - lax.axis_index("dp") * caps_dev
    mine = jnp.arange(caps_dev, dtype=jnp.int32)
    own = jnp.sum((local_rows[:, :, None] == mine[None, None, :]).astype(jnp.float32), axis=1)
    block_scores = (
        jnp.dot(
            caption_hat,
            lax.all_gather(video_hat, "dp", axis=0, tiled=True).T,
            preferred_element_type=jnp.float32,
        )
        * INV_TEMP
    )
    colsum = jnp.sum(jnp.exp(block_scores), axis=1)
    scaled = (caption_hat.astype(jnp.float32) / colsum[:, None]).astype(jnp.bfloat16)
    unit_piece = lax.all_gather(caption_hat, "dp", axis=0, tiled=True)
    scaled_piece = lax.all_gather(scaled, "dp", axis=0, tiled=True)
    block_scores = jnp.dot(video_hat, unit_piece.T, preferred_element_type=jnp.float32) * INV_TEMP
    block_expo = jnp.exp(block_scores)
    block_weights = block_expo.astype(jnp.bfloat16)
    total = jnp.sum(block_expo, axis=1)
    a_sum = jnp.dot(block_weights, unit_piece, preferred_element_type=jnp.float32)
    b_sum = jnp.dot(block_weights, scaled_piece, preferred_element_type=jnp.float32)
    local_scores = jnp.dot(video_hat, caption_hat.T, preferred_element_type=jnp.float32) * INV_TEMP
    local_expo = jnp.exp(local_scores)
    positive = jnp.sum(own * local_expo, axis=1)
    text_part = jnp.sum(own * (jnp.log(colsum)[None, :] - local_scores), axis=1)
    clip_loss = jnp.log(total) - jnp.log(positive) + 0.2 * text_part
    pos_sum = jnp.dot(
        (own * local_expo).astype(jnp.bfloat16), caption_hat, preferred_element_type=jnp.float32
    )
    own_sum = jnp.dot(own.astype(jnp.bfloat16), caption_hat, preferred_element_type=jnp.float32)
    grad = INV_TEMP * (
        a_sum / total[:, None] - pos_sum / positive[:, None] + 0.2 * (b_sum - own_sum)
    )
    grad_video = ((grad - vunit * jnp.sum(vunit * grad, axis=1, keepdims=True)) / vnorm).astype(
        jnp.bfloat16
    )
    grad_pooled = jnp.dot(grad_video, proj_weight.T, preferred_element_type=jnp.float32)
    spread = jnp.broadcast_to(grad_pooled[:, None, None, :] / (frames * pix), pre.shape)
    grad_pre = act_back(spread)[0].astype(jnp.bfloat16)
    grad_in = temporal_back(grad_pre, time_weight)
    rms = jnp.sqrt(jnp.mean(grad_in * grad_in, axis=(1, 2, 3), keepdims=True) + 1e-06)
    new_delta = (delta0 + grad_in / rms).astype(jnp.bfloat16)
    return (new_delta, clip_loss)


def solution(mesh):
    in_specs = (
        P(("groups", "dp"), None, None, None),
        P(("groups", "dp")),
        P(),
        P(),
        P(("groups", "dp"), None),
        P(("groups", "dp"), None),
    )
    out_specs = (P(("groups", "dp"), None, None, None), P(("groups", "dp")))
    return jax.shard_map(shards, mesh=mesh, in_specs=in_specs, out_specs=out_specs, check_vma=False)
```

profile of v0, /device:TPU:0, one launch (start us, length us, event | category | flops | bytes accessed | tf_op | source)
XLA Modules:
  0.0 102.4 jit_solution(11251730279128082261)
XLA Ops:
  0.6 0.0 copy-start
  0.6 0.7 broadcast_multiply_fusion.2
  1.4 0.9 fusion.45
  2.3 0.7 broadcast_subtract_fusion
  3.0 0.1 copy.15
  3.1 0.1 convert_reduce_fusion
  3.1 0.8 fusion.46
  4.0 0.8 fusion.80
  4.8 24.1 %all-gather = bf16[16,20,512]{2,1,0:T(8,128)(2,1)S(1)} all-gather(bf16[1,20,512]{2,1,0:T(8,128)(2,1)S(1)} %fusion.80), channel_id=1, replica_groups=mesh['groups'=2,'dp'=16] {'dp'}, dimensions={0}, use_global_device_ids=true | all-gather | bytes 348160 | tf_op jit(solution)/shard_map/all_gather | solution.py:83
  28.9 0.1 reshape.72
  29.0 0.0 slice-start
  29.0 0.2 add_multiply_fusion.1
  29.2 0.0 slice-start.1
  29.2 0.0 copy-start.2
  29.2 5.5 %fusion.18 = f32[4,4,49,1024]{3,2,1,0:T(8,128)S(1)} fusion(bf16[3,1024,1024]{2,1,0:T(8,128)(2,1)} %param.8, bf16[4,4,49,1024]{3,1,2,0:T(4,128)(2,1)} %param.6, s32[4,49,1024]{2,1,0:T(8,128)S(1)} %add_multiply_fusion.1, s32[4]{0:T(128)S(1)} %broadcast_multiply_fusion.2), kind=kOutput, calls=%fused_computation.28 | convolution fusion | flops 1245167616 | bytes 7716880 | tf_op jit(solution)/shard_map/dot_general | solution.py:31
  34.8 0.0 slice-done
  34.8 0.0 slice-done.1
  34.8 0.0 copy-done.2
  34.8 3.0 %fusion.22 = f32[4,4,49,1024]{3,2,1,0:T(8,128)S(1)} fusion(bf16[3,1024,1024]{2,1,0:T(8,128)(2,1)S(1)} %bitcast.54, bf16[4,4,49,1024]{3,1,2,0:T(4,128)(2,1)S(1)} %copy-done.2, s32[4,49,1024]{2,1,0:T(8,128)S(1)} %add_multiply_fusion.1, s32[4]{0:T(128)S(1)} %broadcast_multiply_fusion.2), kind=kOutput, calls=%fused_computation.32 | convolution fusion | flops 1245167616 | bytes 7832064 | tf_op jit(solution)/shard_map/dot_general | solution.py:31
  37.8 0.0 copy-start.1
  37.8 6.3 %fusion.15 = (f32[4,1024]{1,0:T(4,128)S(1)}, f32[4,4,49,1024]{3,2,1,0:T(8,128)}) fusion(f32[4,4,49,1024]{3,2,1,0:T(8,128)S(1)} %fusion.22, f32[4,4,49,1024]{3,2,1,0:T(8,128)S(1)} %fusion.18, bf16[3,1024,1024]{2,1,0:T(8,128)(2,1)S(1)} %bitcast.54, bf16[4,4,49,1024]{3,1,2,0:T(4,128)(2,1)S(1)} %copy-done.2, s32[4,49,1024]{2,1,0:T(8,128)S(1)} %add_multiply_fusion.1, ...), kind=kOutput, calls=%fused_computation.23 | convolution fusion | flops 1665036288 | bytes 15188480 | tf_op jit(solution)/shard_map/dot_general | solution.py:31
  44.1 0.0 copy-done
  44.2 0.4 multiply_reduce_fusion.2
  44.5 0.3 fusion.67
  44.9 0.2 convolution_divide_fusion.1
  45.0 0.1 convert_bitcast_fusion
  45.1 17.6 %all-gather.1 = bf16[16,4,512]{2,1,0:T(4,128)(2,1)S(1)} all-gather(bf16[1,4,512]{2,1,0:T(4,128)(2,1)S(1)} %convert_bitcast_fusion), channel_id=1, replica_groups=mesh['groups'=2,'dp'=16] {'dp'}, dimensions={0}, use_global_device_ids=true | all-gather | bytes 69632 | tf_op jit(solution)/shard_map/all_gather | solution.py:76
  62.7 0.2 fusion.43
  63.0 0.3 multiply_reduce_fusion.3
  63.3 0.5 multiply_add_fusion
  63.8 0.1 fusion.42
  63.9 0.0 copy-done.1
  63.9 0.1 fusion.47
  64.0 20.1 %all-gather.2 = bf16[16,20,512]{2,1,0:T(8,128)(2,1)S(1)} all-gather(bf16[1,20,512]{2,1,0:T(8,128)(2,1)S(1)} %fusion.47), channel_id=1, replica_groups=mesh['groups'=2,'dp'=16] {'dp'}, dimensions={0}, use_global_device_ids=true | all-gather | bytes 348160 | tf_op jit(solution)/shard_map/all_gather | solution.py:84
  84.1 0.1 reshape.76
  84.2 0.1 fusion.55
  84.3 0.2 multiply_reduce_fusion.1
  84.6 0.0 slice-start.2
  84.6 0.4 broadcast_multiply_fusion
  85.0 0.0 slice-start.3
  85.0 0.0 copy-start.3
  85.0 5.8 %fusion.16 = f32[4,4,49,1024]{3,2,1,0:T(8,128)S(1)} fusion(bf16[3,1024,1024]{2,1,0:T(8,128)(2,1)} %param.8, f32[4,4,49,1024]{3,2,1,0:T(8,128)} %get-tuple-element.15, f32[4,1024]{1,0:T(4,128)S(1)} %get-tuple-element.13, f32[4,1024]{1,0:T(4,128)S(1)} %get-tuple-element.12), kind=kOutput, calls=%fused_computation.26 | convolution fusion | flops 1248378880 | bytes 9011200 | tf_op jit(solution)/shard_map/dot_general | solution.py:44
  90.8 0.0 slice-done.2
  90.8 0.0 slice-done.3
  90.8 0.0 copy-done.3
  90.8 3.2 %fusion.20 = f32[4,4,49,1024]{3,2,1,0:T(8,128)S(1)} fusion(bf16[3,1024,1024]{2,1,0:T(8,128)(2,1)S(1)} %bitcast.56, f32[4,4,49,1024]{3,2,1,0:T(8,128)S(1)} %copy-done.3, f32[4,1024]{1,0:T(4,128)S(1)} %get-tuple-element.13, f32[4,1024]{1,0:T(4,128)S(1)} %get-tuple-element.12), kind=kOutput, calls=%fused_computation.30 | convolution fusion | flops 1248378880 | bytes 9011200 | tf_op jit(solution)/shard_map/dot_general | solution.py:44
  94.1 4.1 %multiply_reduce_fusion = (f32[4]{0:T(128)S(1)}, f32[4,4,49,1024]{3,2,1,0:T(8,128)S(1)}) fusion(f32[4,4,49,1024]{3,2,1,0:T(8,128)S(1)} %fusion.20, f32[4,4,49,1024]{3,2,1,0:T(8,128)S(1)} %fusion.16, bf16[3,1024,1024]{2,1,0:T(8,128)(2,1)S(1)} %bitcast.56, f32[4,4,49,1024]{3,2,1,0:T(8,128)S(1)} %copy-done.3, f32[4,1024]{1,0:T(4,128)S(1)} %get-tuple-element.13, ...), kind=kOutput, calls=%fused_computation.19 | convolution fusion | flops 1662631936 | bytes 16351248 | tf_op jit(solution)/shard_map/dot_general | solution.py:44
  98.2 1.8 %add_convert_fusion = bf16[4,4,49,1024]{3,2,1,0:T(8,128)(2,1)S(1)} fusion(f32[4,4,49,1024]{3,2,1,0:T(8,128)S(1)} %get-tuple-element.24, f32[4]{0:T(128)S(1)} %add_sqrt_fusion, s32[4,49,1024]{2,1,0:T(8,128)S(1)} %add_multiply_fusion.1, s32[4]{0:T(128)S(1)} %broadcast_multiply_fusion.2), kind=kLoop, calls=%fused_computation.18 | loop fusion | flops 12042240 | bytes 5619744 | tf_op jit(solution)/shard_map/convert_element_type | solution.py:111
  100.0 2.4 %copy.16 = bf16[4,4,49,1024]{3,1,2,0:T(4,128)(2,1)} copy(bf16[4,4,49,1024]{3,2,1,0:T(8,128)(2,1)S(1)} %add_convert_fusion) | data formatting | bytes 3211264
  (8 shorter events, 0.1 us)
Async XLA Ops:
  0.6 43.5 %copy-start = (bf16[1024,512]{1,0:T(8,128)(2,1)S(1)}, bf16[1024,512]{1,0:T(8,128)(2,1)}, u32[]{:S(2)}) copy-start(bf16[1024,512]{1,0:T(8,128)(2,1)} %param.9) | copy-start | bytes 3145732
  29.0 5.8 %slice-start = ((s8[6291456]{0:T(1024)(128)(4,1)}), s8[4194304]{0:T(1024)(128)(4,1)S(1)}, s32[]{:S(2)}) async-start(s8[6291456]{0:T(1024)(128)(4,1)} %bitcast.53), calls=%async_computation | async-start | bytes 8388608
  29.2 5.6 %slice-start.1 = ((s8[6291456]{0:T(1024)(128)(4,1)}), s8[2097152]{0:T(1024)(128)(4,1)S(1)}, s32[]{:S(2)}) async-start(s8[6291456]{0:T(1024)(128)(4,1)} %bitcast.53), calls=%async_computation.1 | async-start | bytes 4194304
  29.2 5.6 %copy-start.2 = (bf16[4,4,49,1024]{3,1,2,0:T(4,128)(2,1)S(1)}, bf16[4,4,49,1024]{3,1,2,0:T(4,128)(2,1)}, u32[]{:S(2)}) copy-start(bf16[4,4,49,1024]{3,1,2,0:T(4,128)(2,1)} %param.6) | copy-start | bytes 4816900
  37.8 26.1 %copy-start.1 = (bf16[20,512]{1,0:T(8,128)(2,1)S(1)}, bf16[20,512]{1,0:T(8,128)(2,1)}, u32[]{:S(2)}) copy-start(bf16[20,512]{1,0:T(8,128)(2,1)} %param.10) | copy-start | bytes 61444
  84.6 6.2 %slice-start.2 = ((s8[6291456]{0:T(1024)(128)(4,1)}), s8[4194304]{0:T(1024)(128)(4,1)S(1)}, s32[]{:S(2)}) async-start(s8[6291456]{0:T(1024)(128)(4,1)} %bitcast.55), calls=%async_computation.2 | async-start | bytes 8388608
  85.0 5.8 %slice-start.3 = ((s8[6291456]{0:T(1024)(128)(4,1)}), s8[2097152]{0:T(1024)(128)(4,1)S(1)}, s32[]{:S(2)}) async-start(s8[6291456]{0:T(1024)(128)(4,1)} %bitcast.55), calls=%async_computation.3 | async-start | bytes 4194304
  85.0 5.8 %copy-start.3 = (f32[4,4,49,1024]{3,2,1,0:T(8,128)S(1)}, f32[4,4,49,1024]{3,2,1,0:T(8,128)}, u32[]{:S(2)}) copy-start(f32[4,4,49,1024]{3,2,1,0:T(8,128)} %get-tuple-element.15) | copy-start | bytes 9633796
where the time goes:
time: 103 us; the launch traced here: 102 us
  blocking collectives  61.8 us (60%)
  matrix products  30.3 us (29%)
  other arithmetic  6.73 us (7%)
  local copies, waits for them, and re-layouts  2.72 us (3%)
    all_gather x1, blocking collectives, shards(): unit_piece = lax.all_gather(caption_hat, 'dp', axis=0, tiled=True)  24.1 us
    all_gather x1, blocking collectives, shards(): scaled_piece = lax.all_gather(scaled, 'dp', axis=0, tiled=True)  20.1 us
    all_gather x1, blocking collectives, shards(): lax.all_gather(video_hat, 'dp', axis=0, tiled=True)  17.6 us
    dot_general x3, matrix products, temporal(): jnp.dot(window, time_weight[k], preferred_element_type=jnp.float32)  14.9 us
    dot_general x3, matrix products, temporal_back(): jnp.dot(window, time_weight[k].T, preferred_element_type=jnp.float32)  13.1 us
    unnamed x20, local copies, waits for them, and re-layouts  2.62 us

commit v1 on v0

--- a/solution.py
+++ b/solution.py
@@ -4,6 +4,16 @@
 from jax.sharding import PartitionSpec as P
 
 INV_TEMP = 1.0 / 0.07
+
+
+def leaves_map(shard_in, chunk, axis_id):
+    return jnp.split(
+        lax.all_gather(
+            jnp.concatenate([shard_in, chunk], axis=1), axis_name=axis_id, axis=0, tiled=True
+        ),
+        [shard_in.shape[1]],
+        axis=1,
+    )
 
 
 def sign_field(seeds, frames, pix, chans):
@@ -80,8 +90,7 @@
     )
     colsum = jnp.sum(jnp.exp(block_scores), axis=1)
     scaled = (caption_hat.astype(jnp.float32) / colsum[:, None]).astype(jnp.bfloat16)
-    unit_piece = lax.all_gather(caption_hat, "dp", axis=0, tiled=True)
-    scaled_piece = lax.all_gather(scaled, "dp", axis=0, tiled=True)
+    unit_piece, scaled_piece = leaves_map(caption_hat, scaled, "dp")
     block_scores = jnp.dot(video_hat, unit_piece.T, preferred_element_type=jnp.float32) * INV_TEMP
     block_expo = jnp.exp(block_scores)
     block_weights = block_expo.astype(jnp.bfloat16)

time: 103 us -> 82.9 us (0.80)
  blocking collectives: 61.8 us -> 43 us
    all_gather x2 -> x1, blocking collectives: 44.2 us -> 19.8 us  [leaves_map(): lax.all_gather(jnp.concatenate([shard_in, chunk], axis=1), axis_name=axis...]
    all_gather x1, blocking collectives: 17.6 us -> 23.3 us  [shards(): lax.all_gather(video_hat, 'dp', axis=0, tiled=True)]
    unnamed x20 -> x19, local copies, waits for them, and re-layouts: 2.62 us -> 2.61 us
where the time goes in v1:
time: 82.9 us; the launch traced here: 82.6 us
  blocking collectives  43 us (52%)
  matrix products  30.1 us (36%)
  other arithmetic  5.93 us (7%)
  local copies, waits for them, and re-layouts  2.71 us (3%)
  between operations  0.84 us (1%)
    all_gather x1, blocking collectives, shards(): lax.all_gather(video_hat, 'dp', axis=0, tiled=True)  23.3 us
    all_gather x1, blocking collectives, leaves_map(): lax.all_gather(jnp.concatenate([shard_in, chunk], axis=1), axis_name=axis...  19.8 us
    dot_general x3, matrix products, temporal(): jnp.dot(window, time_weight[k], preferred_element_type=jnp.float32)  14.8 us
    dot_general x3, matrix products, temporal_back(): jnp.dot(window, time_weight[k].T, preferred_element_type=jnp.float32)  13 us
    unnamed x19, local copies, waits for them, and re-layouts  2.61 us
    convert_element_type x1, other arithmetic, shards(): new_delta = (delta0 + grad_in / rms).astype(jnp.bfloat16)  1.83 us

profile of v1, /device:TPU:0, one launch (start us, length us, event | category | flops | bytes accessed | tf_op | source)
XLA Modules:
  0.0 82.6 jit_solution(12380686003961418188)
XLA Ops:
  0.6 0.0 copy-start
  0.6 0.7 broadcast_multiply_fusion.2
  1.4 0.9 %fusion.49 = f32[20]{0:T(128)S(1)} fusion(bf16[20,512]{1,0:T(8,128)(2,1)} %param.10), kind=kLoop, calls=%fused_computation.64 | loop fusion | flops 30700 | bytes 20560 | tf_op jit(solution)/shard_map/reduce_sum | solution.py:77
  2.3 0.7 broadcast_subtract_fusion
  3.0 0.1 copy.15
  3.1 0.1 convert_reduce_fusion
  3.1 0.8 fusion.50
  4.0 0.0 slice-start
  4.0 0.2 add_multiply_fusion.1
  4.1 0.0 slice-start.1
  4.2 0.0 copy-start.2
  4.2 5.5 %fusion.18 = f32[4,4,49,1024]{3,2,1,0:T(8,128)S(1)} fusion(bf16[3,1024,1024]{2,1,0:T(8,128)(2,1)} %param.8, bf16[4,4,49,1024]{3,1,2,0:T(4,128)(2,1)} %param.6, s32[4,49,1024]{2,1,0:T(8,128)S(1)} %add_multiply_fusion.1, s32[4]{0:T(128)S(1)} %broadcast_multiply_fusion.2), kind=kOutput, calls=%fused_computation.28 | convolution fusion | flops 1245167616 | bytes 7716880 | tf_op jit(solution)/shard_map/dot_general | solution.py:41
  9.7 0.0 slice-done
  9.7 0.0 slice-done.1
  9.7 0.0 copy-done.2
  9.7 3.0 %fusion.22 = f32[4,4,49,1024]{3,2,1,0:T(8,128)S(1)} fusion(bf16[3,1024,1024]{2,1,0:T(8,128)(2,1)S(1)} %bitcast.49, bf16[4,4,49,1024]{3,1,2,0:T(4,128)(2,1)S(1)} %copy-done.2, s32[4,49,1024]{2,1,0:T(8,128)S(1)} %add_multiply_fusion.1, s32[4]{0:T(128)S(1)} %broadcast_multiply_fusion.2), kind=kOutput, calls=%fused_computation.32 | convolution fusion | flops 1245167616 | bytes 7832064 | tf_op jit(solution)/shard_map/dot_general | solution.py:41
  12.7 0.0 copy-start.1
  12.7 6.3 %fusion.15 = (f32[4,1024]{1,0:T(4,128)S(1)}, f32[4,4,49,1024]{3,2,1,0:T(8,128)}) fusion(f32[4,4,49,1024]{3,2,1,0:T(8,128)S(1)} %fusion.22, f32[4,4,49,1024]{3,2,1,0:T(8,128)S(1)} %fusion.18, bf16[3,1024,1024]{2,1,0:T(8,128)(2,1)S(1)} %bitcast.49, bf16[4,4,49,1024]{3,1,2,0:T(4,128)(2,1)S(1)} %copy-done.2, s32[4,49,1024]{2,1,0:T(8,128)S(1)} %add_multiply_fusion.1, ...), kind=kOutput, calls=%fused_computation.23 | convolution fusion | flops 1665036288 | bytes 15188480 | tf_op jit(solution)/shard_map/dot_general | solution.py:41
  19.0 0.0 copy-done
  19.0 0.4 multiply_reduce_fusion.2
  19.4 0.1 convert_bitcast_fusion
  19.5 23.3 %all-gather = bf16[16,4,512]{2,1,0:T(4,128)(2,1)S(1)} all-gather(bf16[1,4,512]{2,1,0:T(4,128)(2,1)S(1)} %convert_bitcast_fusion), channel_id=1, replica_groups=mesh['groups'=2,'dp'=16] {'dp'}, dimensions={0}, use_global_device_ids=true | all-gather | bytes 69632 | tf_op jit(solution)/shard_map/all_gather | solution.py:86
  42.7 0.2 fusion.43
  43.0 0.3 multiply_reduce_fusion.3
  43.3 0.0 copy-done.1
  43.3 0.1 divide_convert_fusion
  43.4 19.8 %all-gather.1 = bf16[16,20,1024]{2,1,0:T(8,128)(2,1)S(1)} all-gather(bf16[1,20,1024]{2,1,0:T(8,128)(2,1)S(1)} %maximum_bitcast_fusion), channel_id=1, replica_groups=mesh['groups'=2,'dp'=16] {'dp'}, dimensions={0}, use_global_device_ids=true | all-gather | bytes 696320 | tf_op jit(solution)/shard_map/all_gather | solution.py:11
  63.2 0.1 reshape.74
  63.3 0.3 fusion.69
  63.7 0.5 multiply_add_fusion
  64.2 0.2 convolution_divide_fusion.1
  64.4 0.2 fusion.45
  64.5 0.1 fusion.42
  64.6 0.2 multiply_reduce_fusion.1
  64.9 0.0 slice-start.2
  64.9 0.4 broadcast_multiply_fusion
  65.3 0.0 slice-start.3
  65.3 0.0 copy-start.3
  65.3 5.8 %fusion.16 = f32[4,4,49,1024]{3,2,1,0:T(8,128)S(1)} fusion(bf16[3,1024,1024]{2,1,0:T(8,128)(2,1)} %param.8, f32[4,4,49,1024]{3,2,1,0:T(8,128)} %get-tuple-element.15, f32[4,1024]{1,0:T(4,128)S(1)} %get-tuple-element.13, f32[4,1024]{1,0:T(4,128)S(1)} %get-tuple-element.12), kind=kOutput, calls=%fused_computation.26 | convolution fusion | flops 1248378880 | bytes 9011200 | tf_op jit(solution)/shard_map/dot_general | solution.py:54
  71.1 0.0 slice-done.2
  71.1 0.0 slice-done.3
  71.1 0.0 copy-done.3
  71.1 3.2 %fusion.20 = f32[4,4,49,1024]{3,2,1,0:T(8,128)S(1)} fusion(bf16[3,1024,1024]{2,1,0:T(8,128)(2,1)S(1)} %bitcast.51, f32[4,4,49,1024]{3,2,1,0:T(8,128)S(1)} %copy-done.3, f32[4,1024]{1,0:T(4,128)S(1)} %get-tuple-element.13, f32[4,1024]{1,0:T(4,128)S(1)} %get-tuple-element.12), kind=kOutput, calls=%fused_computation.30 | convolution fusion | flops 1248378880 | bytes 9011200 | tf_op jit(solution)/shard_map/dot_general | solution.py:54
  74.3 4.0 %multiply_reduce_fusion = (f32[4]{0:T(128)S(1)}, f32[4,4,49,1024]{3,2,1,0:T(8,128)S(1)}) fusion(f32[4,4,49,1024]{3,2,1,0:T(8,128)S(1)} %fusion.20, f32[4,4,49,1024]{3,2,1,0:T(8,128)S(1)} %fusion.16, bf16[3,1024,1024]{2,1,0:T(8,128)(2,1)S(1)} %bitcast.51, f32[4,4,49,1024]{3,2,1,0:T(8,128)S(1)} %copy-done.3, f32[4,1024]{1,0:T(4,128)S(1)} %get-tuple-element.13, ...), kind=kOutput, calls=%fused_computation.19 | convolution fusion | flops 1662631936 | bytes 16351248 | tf_op jit(solution)/shard_map/dot_general | solution.py:54
  78.3 1.8 %add_convert_fusion = bf16[4,4,49,1024]{3,2,1,0:T(8,128)(2,1)S(1)} fusion(f32[4,4,49,1024]{3,2,1,0:T(8,128)S(1)} %get-tuple-element.24, f32[4]{0:T(128)S(1)} %add_sqrt_fusion, s32[4,49,1024]{2,1,0:T(8,128)S(1)} %add_multiply_fusion.1, s32[4]{0:T(128)S(1)} %broadcast_multiply_fusion.2), kind=kLoop, calls=%fused_computation.18 | loop fusion | flops 12042240 | bytes 5619744 | tf_op jit(solution)/shard_map/convert_element_type | solution.py:120
  80.2 2.4 %copy.16 = bf16[4,4,49,1024]{3,1,2,0:T(4,128)(2,1)} copy(bf16[4,4,49,1024]{3,2,1,0:T(8,128)(2,1)S(1)} %add_convert_fusion) | data formatting | bytes 3211264
  (9 shorter events, 0.1 us)
Async XLA Ops:
  0.6 18.4 %copy-start = (bf16[1024,512]{1,0:T(8,128)(2,1)S(1)}, bf16[1024,512]{1,0:T(8,128)(2,1)}, u32[]{:S(2)}) copy-start(bf16[1024,512]{1,0:T(8,128)(2,1)} %param.9) | copy-start | bytes 3145732
  4.0 5.7 %slice-start = ((s8[6291456]{0:T(1024)(128)(4,1)}), s8[4194304]{0:T(1024)(128)(4,1)S(1)}, s32[]{:S(2)}) async-start(s8[6291456]{0:T(1024)(128)(4,1)} %bitcast.48), calls=%async_computation | async-start | bytes 8388608
  4.1 5.6 %slice-start.1 = ((s8[6291456]{0:T(1024)(128)(4,1)}), s8[2097152]{0:T(1024)(128)(4,1)S(1)}, s32[]{:S(2)}) async-start(s8[6291456]{0:T(1024)(128)(4,1)} %bitcast.48), calls=%async_computation.1 | async-start | bytes 4194304
  4.2 5.6 %copy-start.2 = (bf16[4,4,49,1024]{3,1,2,0:T(4,128)(2,1)S(1)}, bf16[4,4,49,1024]{3,1,2,0:T(4,128)(2,1)}, u32[]{:S(2)}) copy-start(bf16[4,4,49,1024]{3,1,2,0:T(4,128)(2,1)} %param.6) | copy-start | bytes 4816900
  12.7 30.6 %copy-start.1 = (bf16[20,512]{1,0:T(8,128)(2,1)S(1)}, bf16[20,512]{1,0:T(8,128)(2,1)}, u32[]{:S(2)}) copy-start(bf16[20,512]{1,0:T(8,128)(2,1)} %param.10) | copy-start | bytes 61444
  64.9 6.2 %slice-start.2 = ((s8[6291456]{0:T(1024)(128)(4,1)}), s8[4194304]{0:T(1024)(128)(4,1)S(1)}, s32[]{:S(2)}) async-start(s8[6291456]{0:T(1024)(128)(4,1)} %bitcast.50), calls=%async_computation.2 | async-start | bytes 8388608
  65.3 5.8 %slice-start.3 = ((s8[6291456]{0:T(1024)(128)(4,1)}), s8[2097152]{0:T(1024)(128)(4,1)S(1)}, s32[]{:S(2)}) async-start(s8[6291456]{0:T(1024)(128)(4,1)} %bitcast.50), calls=%async_computation.3 | async-start | bytes 4194304
  65.3 5.8 %copy-start.3 = (f32[4,4,49,1024]{3,2,1,0:T(8,128)S(1)}, f32[4,4,49,1024]{3,2,1,0:T(8,128)}, u32[]{:S(2)}) copy-start(f32[4,4,49,1024]{3,2,1,0:T(8,128)} %get-tuple-element.15) | copy-start | bytes 9633796
